TPU v7x, 256 devices: a whole 4x4x8 slice. The times are simulated.
256 devices in a mesh: leaf: 64 (over z, y, core), rhs: 4 (over x).
Axes of the slice: x: 4, y: 4, z: 8, core: 2. Of those that a mesh axis runs over, the one named last changes fastest.
Arguments:
- densities: bfloat16 [64, 262144], P('rhs', 'leaf'), may hold values from -6 to 6
- bases: float32 [32, 262144], P(None, 'leaf'), may hold values from -0.5 to 0.5
- near_blocks: bfloat16 [2048, 8, 128, 128], P('leaf', 'rhs'), may hold values from -0.1875 to 0.1875
- near_src: int32 [2048, 8], P('leaf', 'rhs'), may hold values from 0 to 55, as said below
- send_leaf: int32 [64, 6, 4], replicated, may hold values from -1 to 31, as said below
- far_src: int32 [2048, 8], P('leaf'), may hold values from 0 to 31
- leaf_coupling: float32 [2048, 8, 32, 32], P('leaf'), may hold values from -0.375 to 0.375
- local_transfer: float32 [64, 64, 32, 32], P('leaf'), may hold values from -0.75 to 0.75
- upper_transfer: float32 [128, 32, 32], replicated, may hold values from -0.75 to 0.75
- up_coupling: float32 [128, 3, 32, 32], replicated, may hold values from -8 to 8
Outputs:
- product: float32 [64, 262144], P('rhs', 'leaf')
Inputs may be any that keep to these rules, and one draw needn't show every extreme that they name: `send_leaf`: entry [e, j, c] is a leaf of device e (local index) whose panel e sends to its face neighbour e + o_j, or -1. Only existing face neighbours receive; the leaves of [e, j] are distinct and come before the -1 entries; every device sends exactly 4 leaves to at least one neighbour, among them its leaf 32 - 1, and exactly 4 to its neighbour at offset -s*s where that exists. `near_src`: A slot of the owner's panel buffer: below 32 a leaf of the same device, else slot 32 + j * 4 + c. It never names an empty slot, and every filled slot is named by some block of the device.
All inputs are finite; a program needn't handle non-finite values.
Results may differ from a plain program's by a relative error of at most 0.0003.
Values may be sent and summed in bfloat16 or wider, within the bound.
A program may use at most 128 MiB of HBM per device.

v0:
```python
import jax
import jax.numpy as jnp
from jax import lax
from jax.sharding import PartitionSpec as P

TOP_PREC = lax.Precision.HIGHEST
FACE_SIGNS = ((1, 0), (-1, 0), (1, 1), (-1, 1), (1, 2), (-1, 2))


def shifted(value, axis, steps):
    count = lax.axis_size(axis)
    first, last = (max(0, -steps), min(count, count - steps))
    return lax.ppermute(value, axis, [(source, source + steps) for source in range(first, last)])


def from_everyone(x, axis):
    copies = jnp.broadcast_to(x, (lax.axis_size(axis), *x.shape))
    return lax.all_to_all(copies, axis, split_axis=0, concat_axis=0, tiled=True)


def laid_out(parts, dim):
    parts = jnp.moveaxis(parts, 0, dim)
    shape = parts.shape
    return parts.reshape(*shape[:dim], shape[dim] * shape[dim + 1], *shape[dim + 2 :])


def gather_directly(x, axis, dim):
    parts = from_everyone(x, axis)
    return laid_out(parts, dim)


def cube_side(device_count):
    return max((edge_len for edge_len in range(1, 65) if edge_len**3 <= device_count))


def face_offsets(device_count):
    side_len = cube_side(device_count)
    return [face_sign * side_len**axis_pos for face_sign, axis_pos in FACE_SIGNS]


def lift_pairs(child_coef, child_maps):
    lifted = jnp.einsum("...nrs,...nqr->...nqs", child_maps, child_coef, precision=TOP_PREC)
    return lifted[..., 0::2, :, :] + lifted[..., 1::2, :, :]


def apply_maps(node_maps, coef_rows):
    return jnp.einsum("...nrs,...nqs->...nqr", node_maps, coef_rows, precision=TOP_PREC)


def couple_level(coef_level, maps_level):
    level_width = coef_level.shape[0]
    even_node = jnp.arange(level_width) % 2 == 0
    padded = jnp.pad(coef_level, ((3, 3), (0, 0), (0, 0)))
    minus_two = padded[1 : level_width + 1]
    plus_two = padded[5 : level_width + 5]
    third_node = jnp.where(
        even_node[:, None, None], padded[6 : level_width + 6], padded[0:level_width]
    )
    first_terms = apply_maps(maps_level[:, 0], minus_two) + apply_maps(maps_level[:, 1], plus_two)
    return first_terms + apply_maps(maps_level[:, 2], third_node)


def upper_tree(roots, upper_transfer, up_coupling):
    node_total = roots.shape[0]
    coef_levels = {node_total: roots}
    level_width = node_total
    while level_width > 4:
        coef_levels[level_width // 2] = lift_pairs(
            coef_levels[level_width], upper_transfer[level_width : 2 * level_width]
        )
        level_width = level_width // 2
    level_field = couple_level(coef_levels[4], up_coupling[4:8])
    level_width = 4
    while level_width < node_total:
        level_width = level_width * 2
        coupled = couple_level(coef_levels[level_width], up_coupling[level_width : 2 * level_width])
        level_field = coupled + apply_maps(
            upper_transfer[level_width : 2 * level_width], jnp.repeat(level_field, 2, axis=0)
        )
    return level_field


def local(
    densities,
    bases,
    near_blocks,
    near_src,
    send_leaf,
    far_src,
    leaf_coupling,
    local_transfer,
    upper_transfer,
    up_coupling,
):
    leaf_devices = lax.axis_size("leaf")
    device_rank = lax.axis_index("leaf")
    columns, points = densities.shape
    leaf_count = near_blocks.shape[0]
    leaf_width = near_blocks.shape[2]
    rank_width = bases.shape[0]
    panels = densities.reshape(columns, leaf_count, leaf_width)
    offsets = face_offsets(leaf_devices)
    arrived = []
    for direction in range(6):
        neighbour_panels = shifted(panels, "leaf", offsets[direction])
        sender = device_rank - offsets[direction]
        inside = (sender >= 0) & (sender < leaf_devices)
        clipped = jnp.clip(sender, 0, leaf_devices - 1)
        sent_leaf = lax.dynamic_index_in_dim(send_leaf, clipped, 0, keepdims=False)[direction]
        chosen = jnp.take(neighbour_panels, jnp.maximum(sent_leaf, 0), axis=1)
        keep_slot = inside & (sent_leaf >= 0)
        arrived.append(jnp.where(keep_slot[None, :, None], chosen, jnp.zeros_like(chosen)))
    buffer = jnp.concatenate([panels] + arrived, axis=1)
    piece_blocks = lax.all_gather(near_blocks, "rhs", axis=1, tiled=True)
    piece_sources = lax.all_gather(near_src, "rhs", axis=1, tiled=True)
    picked = jnp.take(buffer, piece_sources, axis=1)
    near_field = jnp.einsum(
        "tkij,qtkj->qti", piece_blocks, picked, preferred_element_type=jnp.float32
    )
    near_field = near_field.reshape(columns, points)
    basis_view = bases.reshape(rank_width, leaf_count, leaf_width)
    leaf_coef = jnp.einsum(
        "rti,qti->tqr", basis_view, panels.astype(jnp.float32), precision=TOP_PREC
    )
    subtree_maps = local_transfer[0]
    coef_levels = {leaf_count: leaf_coef}
    level_width = leaf_count
    while level_width > 1:
        coef_levels[level_width // 2] = lift_pairs(
            coef_levels[level_width], subtree_maps[level_width : 2 * level_width]
        )
        level_width = level_width // 2
    root_coef = coef_levels[1][0]
    roots = gather_directly(root_coef[None], "leaf", 0)
    root_all = upper_tree(roots, upper_transfer, up_coupling)
    root_field = lax.dynamic_index_in_dim(root_all, device_rank, 0, keepdims=False)
    picked_coef = jnp.take(leaf_coef, far_src, axis=0)
    leaf_local = jnp.einsum("tjrs,tjqs->tqr", leaf_coupling, picked_coef, precision=TOP_PREC)
    level_field = root_field[None]
    level_width = 1
    while level_width < leaf_count:
        level_width = level_width * 2
        level_field = apply_maps(
            subtree_maps[level_width : 2 * level_width], jnp.repeat(level_field, 2, axis=0)
        )
    leaf_field = level_field + leaf_local
    far_part = jnp.einsum("rti,tqr->qti", basis_view, leaf_field, precision=TOP_PREC).reshape(
        columns, points
    )
    return near_field + far_part


def solution(mesh):
    in_specs = (
        P("rhs", "leaf"),
        P(None, "leaf"),
        P("leaf", "rhs", None, None),
        P("leaf", "rhs"),
        P(),
        P("leaf", None),
        P("leaf", None, None, None),
        P("leaf", None, None, None),
        P(),
        P(),
    )
    out_specs = P("rhs", "leaf")
    return jax.shard_map(local, mesh=mesh, in_specs=in_specs, out_specs=out_specs, check_vma=False)
```

profile of v0, /device:TPU:192, one launch (start us, length us, event | category | flops | bytes accessed | tf_op | source)
XLA Modules:
  0.0 177.5 jit_solution(17345306287468822620)
XLA Ops:
  6.5 1.7 copy_bitcast_fusion.1
  8.2 1.9 %collective-permute-start = (bf16[16,32,128]{2,0,1:T(8,128)(2,1)}, bf16[16,32,128]{2,0,1:T(8,128)(2,1)}, u32[]{:S(2)}, u32[]{:S(2)}) collective-permute-start(bf16[16,32,128]{2,0,1:T(8,128)(2,1)} %copy_bitcast_fusion.1), channel_id=1, source_target_pairs={{0,4},{4,8},{8,12},{12,16},{16,20},{20,24},{24,28},{28,32},{32,36}... | collective-permute-start | bytes 393224 | tf_op jit(solution)/shard_map/ppermute | solution.py:13
  10.1 5.8 %collective-permute-start.1 = (bf16[16,32,128]{2,0,1:T(8,128)(2,1)}, bf16[16,32,128]{2,0,1:T(8,128)(2,1)}, u32[]{:S(2)}, u32[]{:S(2)}) collective-permute-start(bf16[16,32,128]{2,0,1:T(8,128)(2,1)} %copy_bitcast_fusion.1), channel_id=1, source_target_pairs={{4,0},{8,4},{12,8},{16,12},{20,16},{24,20},{28,24},{32,28},{36,32}... | collective-permute-start | bytes 393224 | tf_op jit(solution)/shard_map/ppermute | solution.py:13
  15.9 3.0 %collective-permute-start.2 = (bf16[16,32,128]{2,0,1:T(8,128)(2,1)}, bf16[16,32,128]{2,0,1:T(8,128)(2,1)}, u32[]{:S(2)}, u32[]{:S(2)}) collective-permute-start(bf16[16,32,128]{2,0,1:T(8,128)(2,1)} %copy_bitcast_fusion.1), channel_id=1, source_target_pairs={{0,16},{4,20},{8,24},{12,28},{16,32},{20,36},{24,40},{28,44},{32,4... | collective-permute-start | bytes 393224 | tf_op jit(solution)/shard_map/ppermute | solution.py:13
  18.9 5.3 %collective-permute-start.3 = (bf16[16,32,128]{2,0,1:T(8,128)(2,1)}, bf16[16,32,128]{2,0,1:T(8,128)(2,1)}, u32[]{:S(2)}, u32[]{:S(2)}) collective-permute-start(bf16[16,32,128]{2,0,1:T(8,128)(2,1)} %copy_bitcast_fusion.1), channel_id=1, source_target_pairs={{16,0},{20,4},{24,8},{28,12},{32,16},{36,20},{40,24},{44,28},{48,3... | collective-permute-start | bytes 393224 | tf_op jit(solution)/shard_map/ppermute | solution.py:13
  24.1 1.3 collective-permute-start.4
  25.5 1.1 slice.278
  28.0 1.3 copy.156
  33.1 10.9 %all-to-all-start = ((f32[64,1,512]{2,1,0:T(1,128)}), f32[64,1,512]{2,1,0:T(1,128)}, u32[]{:S(2)}, u32[]{:S(2)}) async-start(f32[64,1,512]{2,1,0:T(1,128)} %reshape.311), calls=%async_computation | async-start | bytes 262144 | tf_op jit(solution)/shard_map/all_to_all | solution.py:18
  52.7 10.2 %all-gather = s32[4,2,32]{2,1,0:T(2,128)S(1)} all-gather(s32[1,2,32]{2,1,0:T(2,128)S(1)} %bitcast.205), channel_id=1, replica_groups=mesh['leaf'=64,'rhs'=4] {'rhs'}, dimensions={0}, use_global_device_ids=true | all-gather | bytes 1280 | tf_op jit(solution)/shard_map/all_gather | solution.py:115
  63.7 2.4 %gather_fusion.1 = f32[256,16,32]{2,1,0:T(8,128)} fusion(f32[32,16,32]{2,1,0:T(8,128)S(1)} %fusion.24, s32[1024]{0:T(1024)S(1)} %pad_clamp_fusion), kind=kCustom, calls=%fused_computation.7 | custom fusion | bytes 1049600 | tf_op jit(solution)/shard_map/jit(_take)/gather | solution.py:137
  67.4 1.6 fusion.121
  68.9 1.6 fusion.120
  70.6 1.6 fusion.119
  72.2 1.6 fusion.118
  73.8 1.6 fusion.117
  76.4 4.6 %fusion.2 = f32[32,16,32]{2,1,0:T(8,128)} fusion(f32[32,8,32,32]{3,2,1,0:T(8,128)S(1)} %copy-done.8, f32[32,8,16,32]{3,2,1,0:T(8,128)S(1)} %bitcast.192, pred[32,8]{1,0:T(8,128)(4,1)S(1)} %copy-done.35), kind=kOutput, calls=%fused_computation.10 | convolution fusion | flops 50462720 | bytes 1638656 | tf_op jit(solution)/shard_map/tjrs,tjqs->tqr/dot_general | solution.py:138
  83.7 1.1 slice.319
  86.6 2.4 %copy.161 = f32[32,1,32,32]{3,2,0,1:T(8,128)} copy(f32[32,1,32,32]{0,3,2,1:T(8,128)} %get-tuple-element.32) | data formatting | bytes 262144
  88.9 2.2 %copy.162 = f32[32,1,32,32]{3,2,0,1:T(8,128)} copy(f32[32,1,32,32]{0,3,2,1:T(8,128)} %get-tuple-element.31) | data formatting | bytes 262144
  91.2 1.2 copy.163
  92.4 2.0 %copy.171 = f32[8,1,32,32]{3,2,0,1:T(8,128)} copy(f32[8,1,32,32]{0,3,2,1:T(8,128)} %get-tuple-element.28) | data formatting | bytes 65536
  94.3 2.3 %copy.164 = f32[32,32,32]{2,1,0:T(8,128)} copy(f32[32,32,32]{0,2,1:T(8,128)} %slice.299) | data formatting | bytes 262144
  96.6 1.3 copy.168
  97.9 1.9 %copy.169 = f32[8,1,32,32]{3,2,0,1:T(8,128)} copy(f32[8,1,32,32]{0,3,2,1:T(8,128)} %get-tuple-element.29) | data formatting | bytes 65536
  99.8 1.9 %copy.170 = f32[8,1,32,32]{3,2,0,1:T(8,128)} copy(f32[8,1,32,32]{0,3,2,1:T(8,128)} %get-tuple-element.27) | data formatting | bytes 65536
  101.7 1.9 %copy.175 = f32[4,1,32,32]{3,2,0,1:T(8,128)} copy(f32[4,1,32,32]{0,3,2,1:T(8,128)} %get-tuple-element.26) | data formatting | bytes 32768
  103.9 2.0 %copy.173 = f32[4,1,32,32]{3,2,0,1:T(8,128)} copy(f32[4,1,32,32]{0,3,2,1:T(8,128)} %get-tuple-element.25) | data formatting | bytes 32768
  105.9 2.0 %copy.174 = f32[4,1,32,32]{3,2,0,1:T(8,128)} copy(f32[4,1,32,32]{0,3,2,1:T(8,128)} %get-tuple-element.24) | data formatting | bytes 32768
  107.8 2.0 %copy.167 = f32[16,1,32,32]{3,2,0,1:T(8,128)} copy(f32[16,1,32,32]{0,3,2,1:T(8,128)} %get-tuple-element.22) | data formatting | bytes 131072
  110.7 2.0 %copy.166 = f32[16,1,32,32]{3,2,0,1:T(8,128)} copy(f32[16,1,32,32]{0,3,2,1:T(8,128)} %get-tuple-element.21) | data formatting | bytes 131072
  112.8 2.9 %copy.159 = f32[64,1,32,32]{3,2,0,1:T(8,128)} copy(f32[64,1,32,32]{0,3,2,1:T(8,128)} %get-tuple-element.19) | data formatting | bytes 524288
  115.6 3.0 %copy.158 = f32[64,1,32,32]{3,2,0,1:T(8,128)} copy(f32[64,1,32,32]{0,3,2,1:T(8,128)} %get-tuple-element.20) | data formatting | bytes 524288
  118.7 1.8 copy.157
  121.4 4.2 %collective-permute-start.5 = (bf16[16,32,128]{2,0,1:T(8,128)(2,1)}, bf16[16,32,128]{2,0,1:T(8,128)(2,1)S(1)}, u32[]{:S(2)}, u32[]{:S(2)}) collective-permute-start(bf16[16,32,128]{2,0,1:T(8,128)(2,1)} %copy_bitcast_fusion.1), channel_id=1, source_target_pairs={{64,0},{68,4},{72,8},{76,12},{80,16},{84,20},{88,24},{92,28},{96,3... | collective-permute-start | bytes 393224 | tf_op jit(solution)/shard_map/ppermute | solution.py:13
  125.6 1.6 gather_fusion.2
  127.2 1.6 gather_fusion.3
  128.8 1.6 gather_fusion.4
  130.4 1.6 gather_fusion.5
  132.0 1.6 gather_fusion.6
  138.6 1.8 %gather_fusion = bf16[256,16,128]{2,1,0:T(8,128)(2,1)} fusion(bf16[16,56,128]{2,0,1:T(8,128)(2,1)S(1)} %fusion.88, s32[1024]{0:T(1024)S(1)} %pad_clamp_fusion.1), kind=kCustom, calls=%fused_computation.6 | custom fusion | bytes 2098176 | tf_op jit(solution)/shard_map/jit(_take)/gather | solution.py:116
  140.9 1.8 %reduce.24 = f32[64,512]{1,0:T(8,128)S(1)} reduce(f32[64,1,512]{2,1,0:T(1,128)} %all-to-all-done, f32[]{:T(128)} %broadcast.440), dimensions={1}, to_apply=%all_to_all.3.reduce_sub_computation | reduce | bytes 262148 | tf_op jit(solution)/shard_map/all_to_all | solution.py:18
  144.1 1.8 %fusion.122 = f32[32,16,32]{2,1,0:T(8,128)S(1)} fusion(f32[32,16,32]{2,1,0:T(8,128)S(1)} %slice_add_fusion, f32[32,32,32]{2,1,0:T(8,128)} %copy.164), kind=kOutput, calls=%fused_computation.207 | convolution fusion | flops 6291456 | bytes 262144 | tf_op jit(solution)/shard_map/...nrs,...nqr->...nqs/dot_general | solution.py:42
  155.0 1.8 %fusion.10 = f32[64,16,32]{2,1,0:T(8,128)S(1)} fusion(f32[64,1,32,32]{3,2,0,1:T(8,128)S(1)} %copy-done.6, f32[64,16,32]{2,1,0:T(8,128)S(1)} %bitcast.193, pred[64]{0:T(512)(128)(4,1)S(1)} %copy-done.41), kind=kOutput, calls=%fused_computation.26 | convolution fusion | flops 12615680 | bytes 524352 | tf_op jit(solution)/shard_map/...nrs,...nqs->...nqr/dot_general | solution.py:47
  156.9 1.7 fusion.126
  158.6 2.0 %fusion.12 = f32[64,16,32]{2,1,0:T(8,128)S(1)} fusion(f32[64,1,32,32]{3,2,0,1:T(8,128)S(1)} %copy-done.19, f32[64,1,16,32]{3,2,1,0:T(8,128)S(1)} %reshape.312), kind=kOutput, calls=%fused_computation.28 | convolution fusion | flops 12189696 | bytes 524288 | tf_op jit(solution)/shard_map/...nrs,...nqs->...nqr/dot_general | solution.py:47
  160.6 1.7 fusion.14
  164.6 4.7 %convolution_bitcast_fusion = f32[32,16,128]{2,1,0:T(8,128)S(1)} fusion(bf16[32,8,128,128]{3,2,1,0:T(8,128)(2,1)} %all-gather.3.cloned.1.call-done, bf16[32,8,16,128]{3,2,1,0:T(8,128)(2,1)S(1)} %bitcast.194, pred[32,8]{1,0:T(8,128)(4,1)S(1)} %copy.111), kind=kOutput, calls=%fused_computation.17 | convolution fusion | flops 134742016 | bytes 9699584 | tf_op jit(solution)/shard_map/tkij,qtkj->qti/dot_general | solution.py:117
  (203 shorter events, 42.8 us)
Async XLA Ops:
  6.5 20.8 %copy-start = (f32[32,4096]{1,0:T(8,128)S(1)}, f32[32,4096]{1,0:T(8,128)}, u32[]{:S(2)}) copy-start(f32[32,4096]{1,0:T(8,128)} %param.13) | copy-start | bytes 1572868
  6.5 18.9 %copy-start.2 = (f32[1,64,32,32]{1,3,2,0:T(8,128)S(1)}, f32[1,64,32,32]{1,3,2,0:T(8,128)}, u32[]{:S(2)}) copy-start(f32[1,64,32,32]{1,3,2,0:T(8,128)} %param.19) | copy-start | bytes 786436
  6.5 158.1 %all-gather.3.cloned.1.call-start = ((), (), s32[]{:S(2)}) async-start(), calls=%async_computation.1 | async-start | bytes 10485760 | tf_op jit(solution)/shard_map/all_gather | solution.py:114
  8.2 113.2 %collective-permute-start = (bf16[16,32,128]{2,0,1:T(8,128)(2,1)}, bf16[16,32,128]{2,0,1:T(8,128)(2,1)}, u32[]{:S(2)}, u32[]{:S(2)}) collective-permute-start(bf16[16,32,128]{2,0,1:T(8,128)(2,1)} %copy_bitcast_fusion.1), channel_id=1, source_target_pairs={{0,4},{4,8},{8,12},{12,16},{16,20},{20,24},{24,28},{28,32},{32,36}... | collective-permute-start | bytes 393224 | tf_op jit(solution)/shard_map/ppermute | solution.py:13
  10.1 117.0 %collective-permute-start.1 = (bf16[16,32,128]{2,0,1:T(8,128)(2,1)}, bf16[16,32,128]{2,0,1:T(8,128)(2,1)}, u32[]{:S(2)}, u32[]{:S(2)}) collective-permute-start(bf16[16,32,128]{2,0,1:T(8,128)(2,1)} %copy_bitcast_fusion.1), channel_id=1, source_target_pairs={{4,0},{8,4},{12,8},{16,12},{20,16},{24,20},{28,24},{32,28},{36,32}... | collective-permute-start | bytes 393224 | tf_op jit(solution)/shard_map/ppermute | solution.py:13
  15.9 112.9 %collective-permute-start.2 = (bf16[16,32,128]{2,0,1:T(8,128)(2,1)}, bf16[16,32,128]{2,0,1:T(8,128)(2,1)}, u32[]{:S(2)}, u32[]{:S(2)}) collective-permute-start(bf16[16,32,128]{2,0,1:T(8,128)(2,1)} %copy_bitcast_fusion.1), channel_id=1, source_target_pairs={{0,16},{4,20},{8,24},{12,28},{16,32},{20,36},{24,40},{28,44},{32,4... | collective-permute-start | bytes 393224 | tf_op jit(solution)/shard_map/ppermute | solution.py:13
  18.9 111.5 %collective-permute-start.3 = (bf16[16,32,128]{2,0,1:T(8,128)(2,1)}, bf16[16,32,128]{2,0,1:T(8,128)(2,1)}, u32[]{:S(2)}, u32[]{:S(2)}) collective-permute-start(bf16[16,32,128]{2,0,1:T(8,128)(2,1)} %copy_bitcast_fusion.1), channel_id=1, source_target_pairs={{16,0},{20,4},{24,8},{28,12},{32,16},{36,20},{40,24},{44,28},{48,3... | collective-permute-start | bytes 393224 | tf_op jit(solution)/shard_map/ppermute | solution.py:13
  24.1 107.8 %collective-permute-start.4 = (bf16[16,32,128]{2,0,1:T(8,128)(2,1)}, bf16[16,32,128]{2,0,1:T(8,128)(2,1)}, u32[]{:S(2)}, u32[]{:S(2)}) collective-permute-start(bf16[16,32,128]{2,0,1:T(8,128)(2,1)} %copy_bitcast_fusion.1), channel_id=1, source_target_pairs={{0,64},{4,68},{8,72},{12,76},{16,80},{20,84},{24,88},{28,92},{32,9... | collective-permute-start | bytes 393224 | tf_op jit(solution)/shard_map/ppermute | solution.py:13
  29.6 2.2 %copy-start.21 = (f32[1,4,32,32]{3,2,1,0:T(8,128)}, f32[1,4,32,32]{3,2,1,0:T(8,128)S(1)}, u32[]{:S(2)}) copy-start(f32[1,4,32,32]{3,2,1,0:T(8,128)S(1)} %copy.155) | copy-start | bytes 49156
  29.8 2.3 %copy-start.15 = (f32[1,8,32,32]{3,2,1,0:T(8,128)}, f32[1,8,32,32]{3,2,1,0:T(8,128)S(1)}, u32[]{:S(2)}) copy-start(f32[1,8,32,32]{3,2,1,0:T(8,128)S(1)} %copy.154) | copy-start | bytes 98308
  30.1 13.9 %copy-start.33 = (s32[64,6,4]{0,2,1:T(4,128)S(1)}, s32[64,6,4]{0,2,1:T(4,128)}, u32[]{:S(2)}) copy-start(s32[64,6,4]{0,2,1:T(4,128)} %param.16) | copy-start | bytes 18436
  30.1 22.7 %copy-start.37 = (s32[32,2]{0,1:T(2,128)S(1)}, s32[32,2]{0,1:T(2,128)}, u32[]{:S(2)}) copy-start(s32[32,2]{0,1:T(2,128)} %param.15) | copy-start | bytes 772
  30.6 32.4 %copy-start.34 = (s32[32,8]{0,1:T(8,128)S(1)}, s32[32,8]{0,1:T(8,128)}, u32[]{:S(2)}) copy-start(s32[32,8]{0,1:T(8,128)} %param.17) | copy-start | bytes 3076
  33.1 107.3 %all-to-all-start = ((f32[64,1,512]{2,1,0:T(1,128)}), f32[64,1,512]{2,1,0:T(1,128)}, u32[]{:S(2)}, u32[]{:S(2)}) async-start(f32[64,1,512]{2,1,0:T(1,128)} %reshape.311), calls=%async_computation | async-start | bytes 262144 | tf_op jit(solution)/shard_map/all_to_all | solution.py:18
  63.7 3.7 %copy-start.1 = (f32[128,3,32,32]{0,3,2,1:T(8,128)S(1)}, f32[128,3,32,32]{0,3,2,1:T(8,128)}, u32[]{:S(2)}) copy-start(f32[128,3,32,32]{0,3,2,1:T(8,128)} %param.21) | copy-start | bytes 4718596
  70.6 4.8 %copy-start.35 = (pred[32,8]{1,0:T(8,128)(4,1)S(1)}, pred[32,8]{1,0:T(8,128)(4,1)}, u32[]{:S(2)}) copy-start(pred[32,8]{1,0:T(8,128)(4,1)} %copy.146) | copy-start | bytes 772
  72.2 3.2 %copy-start.8 = (f32[32,8,32,32]{3,2,1,0:T(8,128)S(1)}, f32[32,8,32,32]{3,2,1,0:T(8,128)}, u32[]{:S(2)}) copy-start(f32[32,8,32,32]{3,2,1,0:T(8,128)} %param.18) | copy-start | bytes 3145732
  73.8 2.6 %copy-start.4 = (f32[256,16,32]{2,1,0:T(8,128)S(1)}, f32[256,16,32]{2,1,0:T(8,128)}, u32[]{:S(2)}) copy-start(f32[256,16,32]{2,1,0:T(8,128)} %gather_fusion.1) | copy-start | bytes 1572868
  76.4 5.1 %copy-start.3 = (f32[128,32,32]{0,2,1:T(8,128)S(1)}, f32[128,32,32]{0,2,1:T(8,128)}, u32[]{:S(2)}) copy-start(f32[128,32,32]{0,2,1:T(8,128)} %param.20) | copy-start | bytes 1572868
  81.5 4.0 %copy-start.36 = (pred[32,8]{0,1:T(8,128)(4,1)S(1)}, pred[32,8]{0,1:T(8,128)(4,1)}, u32[]{:S(2)}) copy-start(pred[32,8]{0,1:T(8,128)(4,1)} %compare_and_fusion.1) | copy-start | bytes 772
  86.6 4.6 %copy-start.13 = (f32[32,1,32,32]{0,3,2,1:T(8,128)S(1)}, f32[32,1,32,32]{0,3,2,1:T(8,128)}, u32[]{:S(2)}) copy-start(f32[32,1,32,32]{0,3,2,1:T(8,128)} %get-tuple-element.30) | copy-start | bytes 393220
  92.4 11.3 %copy-start.10 = (f32[8,32,32]{0,2,1:T(8,128)S(1)}, f32[8,32,32]{0,2,1:T(8,128)}, u32[]{:S(2)}) copy-start(f32[8,32,32]{0,2,1:T(8,128)} %slice.319) | copy-start | bytes 98308
  103.9 5.9 %copy-start.12 = (f32[16,1,32,32]{0,3,2,1:T(8,128)S(1)}, f32[16,1,32,32]{0,3,2,1:T(8,128)}, u32[]{:S(2)}) copy-start(f32[16,1,32,32]{0,3,2,1:T(8,128)} %get-tuple-element.23) | copy-start | bytes 196612
  110.7 8.0 %copy-start.11 = (f32[64,1,32,32]{0,3,2,1:T(8,128)S(1)}, f32[64,1,32,32]{0,3,2,1:T(8,128)}, u32[]{:S(2)}) copy-start(f32[64,1,32,32]{0,3,2,1:T(8,128)} %get-tuple-element.18) | copy-start | bytes 786436
  121.4 15.7 %collective-permute-start.5 = (bf16[16,32,128]{2,0,1:T(8,128)(2,1)}, bf16[16,32,128]{2,0,1:T(8,128)(2,1)S(1)}, u32[]{:S(2)}, u32[]{:S(2)}) collective-permute-start(bf16[16,32,128]{2,0,1:T(8,128)(2,1)} %copy_bitcast_fusion.1), channel_id=1, source_target_pairs={{64,0},{68,4},{72,8},{76,12},{80,16},{84,20},{88,24},{92,28},{96,3... | collective-permute-start | bytes 393224 | tf_op jit(solution)/shard_map/ppermute | solution.py:13
  144.0 2.6 %copy-start.31 = (f32[4,1,32,32]{3,2,0,1:T(8,128)S(1)}, f32[4,1,32,32]{3,2,0,1:T(8,128)}, u32[]{:S(2)}) copy-start(f32[4,1,32,32]{3,2,0,1:T(8,128)} %copy.175) | copy-start | bytes 49156
  144.0 2.6 %copy-start.42 = (pred[4]{0:T(512)(128)(4,1)S(1)}, pred[4]{0:T(512)(128)(4,1)}, u32[]{:S(2)}) copy-start(pred[4]{0:T(512)(128)(4,1)} %fusion.105) | copy-start | bytes 16
  144.0 2.9 %copy-start.32 = (f32[4,1,32,32]{3,2,0,1:T(8,128)S(1)}, f32[4,1,32,32]{3,2,0,1:T(8,128)}, u32[]{:S(2)}) copy-start(f32[4,1,32,32]{3,2,0,1:T(8,128)} %copy.173) | copy-start | bytes 49156
  144.0 3.1 %copy-start.30 = (f32[4,1,32,32]{3,2,0,1:T(8,128)S(1)}, f32[4,1,32,32]{3,2,0,1:T(8,128)}, u32[]{:S(2)}) copy-start(f32[4,1,32,32]{3,2,0,1:T(8,128)} %copy.174) | copy-start | bytes 49156
  144.0 3.3 %copy-start.24 = (f32[8,1,32,32]{3,2,0,1:T(8,128)S(1)}, f32[8,1,32,32]{3,2,0,1:T(8,128)}, u32[]{:S(2)}) copy-start(f32[8,1,32,32]{3,2,0,1:T(8,128)} %copy.171) | copy-start | bytes 98308
  144.0 3.3 %copy-start.39 = (pred[8]{0:T(512)(128)(4,1)S(1)}, pred[8]{0:T(512)(128)(4,1)}, u32[]{:S(2)}) copy-start(pred[8]{0:T(512)(128)(4,1)} %fusion.104) | copy-start | bytes 28
  144.0 3.7 %copy-start.25 = (f32[8,1,32,32]{3,2,0,1:T(8,128)S(1)}, f32[8,1,32,32]{3,2,0,1:T(8,128)}, u32[]{:S(2)}) copy-start(f32[8,1,32,32]{3,2,0,1:T(8,128)} %copy.169) | copy-start | bytes 98308
  144.0 4.0 %copy-start.23 = (f32[8,1,32,32]{3,2,0,1:T(8,128)S(1)}, f32[8,1,32,32]{3,2,0,1:T(8,128)}, u32[]{:S(2)}) copy-start(f32[8,1,32,32]{3,2,0,1:T(8,128)} %copy.170) | copy-start | bytes 98308
  144.1 4.6 %copy-start.18 = (f32[16,1,32,32]{3,2,0,1:T(8,128)S(1)}, f32[16,1,32,32]{3,2,0,1:T(8,128)}, u32[]{:S(2)}) copy-start(f32[16,1,32,32]{3,2,0,1:T(8,128)} %copy.167) | copy-start | bytes 196612
  144.1 4.6 %copy-start.40 = (pred[16]{0:T(512)(128)(4,1)S(1)}, pred[16]{0:T(512)(128)(4,1)}, u32[]{:S(2)}) copy-start(pred[16]{0:T(512)(128)(4,1)} %fusion.103) | copy-start | bytes 52
  145.9 3.9 %copy-start.28 = (f32[16,1,32,32]{3,2,0,1:T(8,128)S(1)}, f32[16,1,32,32]{3,2,0,1:T(8,128)}, u32[]{:S(2)}) copy-start(f32[16,1,32,32]{3,2,0,1:T(8,128)} %copy.165) | copy-start | bytes 196612
  146.5 3.8 %copy-start.29 = (f32[16,1,32,32]{3,2,0,1:T(8,128)S(1)}, f32[16,1,32,32]{3,2,0,1:T(8,128)}, u32[]{:S(2)}) copy-start(f32[16,1,32,32]{3,2,0,1:T(8,128)} %copy.166) | copy-start | bytes 196612
  148.1 2.9 %copy-start.26 = (f32[32,1,32,32]{3,2,0,1:T(8,128)S(1)}, f32[32,1,32,32]{3,2,0,1:T(8,128)}, u32[]{:S(2)}) copy-start(f32[32,1,32,32]{3,2,0,1:T(8,128)} %copy.161) | copy-start | bytes 393220
  150.9 1.0 copy-start.27
  152.0 2.1 %copy-start.5 = (f32[32,32,32]{2,1,0:T(8,128)S(1)}, f32[32,32,32]{2,1,0:T(8,128)}, u32[]{:S(2)}) copy-start(f32[32,32,32]{2,1,0:T(8,128)} %copy.164) | copy-start | bytes 393220
  153.0 2.0 %copy-start.6 = (f32[64,1,32,32]{3,2,0,1:T(8,128)S(1)}, f32[64,1,32,32]{3,2,0,1:T(8,128)}, u32[]{:S(2)}) copy-start(f32[64,1,32,32]{3,2,0,1:T(8,128)} %copy.159) | copy-start | bytes 786436
  153.0 2.0 %copy-start.41 = (pred[64]{0:T(512)(128)(4,1)S(1)}, pred[64]{0:T(512)(128)(4,1)}, u32[]{:S(2)}) copy-start(pred[64]{0:T(512)(128)(4,1)} %fusion.101) | copy-start | bytes 196
  155.0 3.6 %copy-start.19 = (f32[64,1,32,32]{3,2,0,1:T(8,128)S(1)}, f32[64,1,32,32]{3,2,0,1:T(8,128)}, u32[]{:S(2)}) copy-start(f32[64,1,32,32]{3,2,0,1:T(8,128)} %copy.158) | copy-start | bytes 786436
  158.6 2.0 %copy-start.20 = (f32[64,1,32,32]{3,2,0,1:T(8,128)S(1)}, f32[64,1,32,32]{3,2,0,1:T(8,128)}, u32[]{:S(2)}) copy-start(f32[64,1,32,32]{3,2,0,1:T(8,128)} %copy.157) | copy-start | bytes 786436
  160.6 1.9 %copy-start.22 = (f32[1,4,32,32]{3,2,1,0:T(8,128)S(1)}, f32[1,4,32,32]{3,2,1,0:T(8,128)}, u32[]{:S(2)}) copy-start(f32[1,4,32,32]{3,2,1,0:T(8,128)} %copy-done.21) | copy-start | bytes 49156
  160.6 2.2 %copy-start.16 = (f32[1,8,32,32]{3,2,1,0:T(8,128)S(1)}, f32[1,8,32,32]{3,2,1,0:T(8,128)}, u32[]{:S(2)}) copy-start(f32[1,8,32,32]{3,2,1,0:T(8,128)} %copy-done.15) | copy-start | bytes 98308
  160.6 3.1 %copy-start.17 = (f32[32,16,32]{2,1,0:T(8,128)S(1)}, f32[32,16,32]{2,1,0:T(8,128)}, u32[]{:S(2)}) copy-start(f32[32,16,32]{2,1,0:T(8,128)} %fusion.2) | copy-start | bytes 196612
  162.3 2.3 %copy-start.7 = (bf16[256,16,128]{2,1,0:T(8,128)(2,1)S(1)}, bf16[256,16,128]{2,1,0:T(8,128)(2,1)}, u32[]{:S(2)}) copy-start(bf16[256,16,128]{2,1,0:T(8,128)(2,1)} %gather_fusion) | copy-start | bytes 3145732
  (3 other events, 3.0 us)
Sparse Core Ops, SparseCore 0:
  25.6 87.3 all-gather.2
where the time goes:
time: 179 us; the launch traced here: 178 us
  local copies, waits for them, and re-layouts  70.7 us (39%)
  matrix products  32.5 us (18%)
  starting transfers between devices  32.2 us (18%)
  other arithmetic  17.6 us (10%)
  between operations  14.3 us (8%)
  blocking collectives  10.2 us (6%)
    unnamed x113, local copies, waits for them, and re-layouts  39.9 us
    ppermute x6, starting transfers between devices, shifted(): lax.ppermute(value, axis, [(source, source + steps) for source in range(f...  21.4 us
    dot_general x24, matrix products, apply_maps(): jnp.einsum('...nrs,...nqs->...nqr', node_maps, coef_rows, precision=TOP_P...  17.2 us
    all_to_all x1, starting transfers between devices, from_everyone(): return lax.all_to_all(copies, axis, split_axis=0, concat_axis=0, tiled=True)  10.9 us
    all_gather x1, blocking collectives, local(): piece_sources = lax.all_gather(near_src, 'rhs', axis=1, tiled=True)  10.2 us
    gather x6, local copies, waits for them, and re-layouts, local(): chosen = jnp.take(neighbour_panels, jnp.maximum(sent_leaf, 0), axis=1)  8.61 us
    dot_general x9, matrix products, lift_pairs(): jnp.einsum('...nrs,...nqr->...nqs', child_maps, child_coef, precision=TOP...  4.9 us
    slice x3, local copies, waits for them, and re-layouts, couple_level(): maps_level[:, 1]  4.84 us
  transfers between devices with their start and end apart: 8, of which 0 were waited for; matrix products, arithmetic and copies ran while one was open for 63% of the time, Pallas kernels for 0%

commit v1 on v0

--- a/solution.py
+++ b/solution.py
@@ -112,7 +112,9 @@
         arrived.append(jnp.where(keep_slot[None, :, None], chosen, jnp.zeros_like(chosen)))
     buffer = jnp.concatenate([panels] + arrived, axis=1)
     piece_blocks = lax.all_gather(near_blocks, "rhs", axis=1, tiled=True)
-    piece_sources = lax.all_gather(near_src, "rhs", axis=1, tiled=True)
+    piece_sources = jnp.concatenate(
+        lax.all_to_all(jnp.stack([near_src] * lax.axis_size("rhs")), "rhs", 0, 0), axis=1
+    )
     picked = jnp.take(buffer, piece_sources, axis=1)
     near_field = jnp.einsum(
         "tkij,qtkj->qti", piece_blocks, picked, preferred_element_type=jnp.float32

time: 179 us -> 183 us (1.022)
  the two profiles are of different devices: /device:TPU:192 before, /device:TPU:10 now
where the time goes in v1:
time: 183 us; the launch traced here: 181 us
  local copies, waits for them, and re-layouts  78.3 us (43%)
  starting transfers between devices  36.4 us (20%)
  matrix products  34.1 us (19%)
  other arithmetic  15.6 us (9%)
  between operations  14.5 us (8%)
  waiting for transfers between devices  2.32 us (1%)
    unnamed x137, local copies, waits for them, and re-layouts  44.4 us
    ppermute x6, starting transfers between devices, shifted(): lax.ppermute(value, axis, [(source, source + steps) for source in range(f...  20.9 us
    dot_general x24, matrix products, apply_maps(): jnp.einsum('...nrs,...nqs->...nqr', node_maps, coef_rows, precision=TOP_P...  17.2 us
    all_to_all x1, starting transfers between devices, from_everyone(): return lax.all_to_all(copies, axis, split_axis=0, concat_axis=0, tiled=True)  10.6 us
    gather x6, local copies, waits for them, and re-layouts, local(): chosen = jnp.take(neighbour_panels, jnp.maximum(sent_leaf, 0), axis=1)  8.61 us
    dot_general x1, matrix products, local(): jnp.einsum('tjrs,tjqs->tqr', leaf_coupling, picked_coef, precision=TOP_PREC)  7.38 us
    and x6, other arithmetic, local(): chosen = jnp.take(neighbour_panels, jnp.maximum(sent_leaf, 0), axis=1)  7.17 us
    slice x5, local copies, waits for them, and re-layouts, local(): subtree_maps[level_width:2 * level_width]  5.01 us
  transfers between devices with their start and end apart: 9, of which 1 were waited for; matrix products, arithmetic and copies ran while one was open for 66% of the time, Pallas kernels for 0%

profile of v1, /device:TPU:10, one launch (start us, length us, event | category | flops | bytes accessed | tf_op | source)
XLA Modules:
  0.0 181.2 jit_solution(10710418139337456034)
XLA Ops:
  6.6 1.6 copy_bitcast_fusion.1
  8.2 1.9 %collective-permute-start = (bf16[16,32,128]{2,0,1:T(8,128)(2,1)}, bf16[16,32,128]{2,0,1:T(8,128)(2,1)}, u32[]{:S(2)}, u32[]{:S(2)}) collective-permute-start(bf16[16,32,128]{2,0,1:T(8,128)(2,1)} %copy_bitcast_fusion.1), channel_id=1, source_target_pairs={{0,4},{4,8},{8,12},{12,16},{16,20},{20,24},{24,28},{28,32},{32,36}... | collective-permute-start | bytes 393224 | tf_op jit(solution)/shard_map/ppermute | solution.py:13
  10.1 3.6 %collective-permute-start.1 = (bf16[16,32,128]{2,0,1:T(8,128)(2,1)}, bf16[16,32,128]{2,0,1:T(8,128)(2,1)}, u32[]{:S(2)}, u32[]{:S(2)}) collective-permute-start(bf16[16,32,128]{2,0,1:T(8,128)(2,1)} %copy_bitcast_fusion.1), channel_id=1, source_target_pairs={{4,0},{8,4},{12,8},{16,12},{20,16},{24,20},{28,24},{32,28},{36,32}... | collective-permute-start | bytes 393224 | tf_op jit(solution)/shard_map/ppermute | solution.py:13
  13.8 4.9 %collective-permute-start.2 = (bf16[16,32,128]{2,0,1:T(8,128)(2,1)}, bf16[16,32,128]{2,0,1:T(8,128)(2,1)}, u32[]{:S(2)}, u32[]{:S(2)}) collective-permute-start(bf16[16,32,128]{2,0,1:T(8,128)(2,1)} %copy_bitcast_fusion.1), channel_id=1, source_target_pairs={{0,16},{4,20},{8,24},{12,28},{16,32},{20,36},{24,40},{28,44},{32,4... | collective-permute-start | bytes 393224 | tf_op jit(solution)/shard_map/ppermute | solution.py:13
  18.7 1.3 collective-permute-start.3
  19.9 8.0 %collective-permute-start.4 = (bf16[16,32,128]{2,0,1:T(8,128)(2,1)}, bf16[16,32,128]{2,0,1:T(8,128)(2,1)}, u32[]{:S(2)}, u32[]{:S(2)}) collective-permute-start(bf16[16,32,128]{2,0,1:T(8,128)(2,1)} %copy_bitcast_fusion.1), channel_id=1, source_target_pairs={{0,64},{4,68},{8,72},{12,76},{16,80},{20,84},{24,88},{28,92},{32,9... | collective-permute-start | bytes 393224 | tf_op jit(solution)/shard_map/ppermute | solution.py:13
  28.5 4.8 %all-to-all-start = ((s32[4,32,2]{1,2,0:T(2,128)}), s32[4,32,2]{1,2,0:T(2,128)S(1)}, u32[]{:S(2)}, u32[]{:S(2)}) async-start(s32[4,32,2]{1,2,0:T(2,128)} %stack.2), calls=%async_computation | async-start | bytes 8192 | tf_op jit(solution)/shard_map/all_to_all | solution.py:116
  38.9 1.6 fusion.121
  40.5 1.6 fusion.120
  44.9 1.6 fusion.119
  48.1 1.6 fusion.118
  50.3 1.6 fusion.117
  57.8 1.9 %copy.156 = f32[1,2,32,32]{3,2,1,0:T(8,128)} copy(f32[1,2,32,32]{1,3,2,0:T(8,128)} %slice.278) | data formatting | bytes 16384
  60.7 2.0 %copy.155 = f32[1,4,32,32]{3,2,1,0:T(8,128)} copy(f32[1,4,32,32]{1,3,2,0:T(8,128)} %slice.274) | data formatting | bytes 32768
  63.5 1.3 copy.153
  64.9 1.5 copy.152
  66.4 2.4 %gather_fusion.1 = f32[256,16,32]{2,1,0:T(8,128)} fusion(f32[32,16,32]{2,1,0:T(8,128)S(1)} %fusion.24, s32[1024]{0:T(1024)S(1)} %pad_clamp_fusion), kind=kCustom, calls=%fused_computation.7 | custom fusion | bytes 1049600 | tf_op jit(solution)/shard_map/jit(_take)/gather | solution.py:139
  71.3 2.2 %copy.161 = f32[32,1,32,32]{3,2,0,1:T(8,128)} copy(f32[32,1,32,32]{0,3,2,1:T(8,128)} %get-tuple-element.32) | data formatting | bytes 262144
  73.6 2.3 %copy.162 = f32[32,1,32,32]{3,2,0,1:T(8,128)} copy(f32[32,1,32,32]{0,3,2,1:T(8,128)} %get-tuple-element.31) | data formatting | bytes 262144
  77.1 2.0 %copy.171 = f32[8,1,32,32]{3,2,0,1:T(8,128)} copy(f32[8,1,32,32]{0,3,2,1:T(8,128)} %get-tuple-element.28) | data formatting | bytes 65536
  79.0 1.5 copy.164
  80.5 2.0 %copy.168 = f32[16,32,32]{2,1,0:T(8,128)} copy(f32[16,32,32]{0,2,1:T(8,128)} %slice.309) | data formatting | bytes 131072
  82.5 1.9 %copy.169 = f32[8,1,32,32]{3,2,0,1:T(8,128)} copy(f32[8,1,32,32]{0,3,2,1:T(8,128)} %get-tuple-element.29) | data formatting | bytes 65536
  84.4 1.9 %copy.170 = f32[8,1,32,32]{3,2,0,1:T(8,128)} copy(f32[8,1,32,32]{0,3,2,1:T(8,128)} %get-tuple-element.27) | data formatting | bytes 65536
  86.3 2.0 %copy.175 = f32[4,1,32,32]{3,2,0,1:T(8,128)} copy(f32[4,1,32,32]{0,3,2,1:T(8,128)} %get-tuple-element.26) | data formatting | bytes 32768
  89.1 2.0 %copy.173 = f32[4,1,32,32]{3,2,0,1:T(8,128)} copy(f32[4,1,32,32]{0,3,2,1:T(8,128)} %get-tuple-element.25) | data formatting | bytes 32768
  91.1 2.0 %copy.174 = f32[4,1,32,32]{3,2,0,1:T(8,128)} copy(f32[4,1,32,32]{0,3,2,1:T(8,128)} %get-tuple-element.24) | data formatting | bytes 32768
  93.1 2.0 %copy.167 = f32[16,1,32,32]{3,2,0,1:T(8,128)} copy(f32[16,1,32,32]{0,3,2,1:T(8,128)} %get-tuple-element.22) | data formatting | bytes 131072
  96.0 2.0 %copy.166 = f32[16,1,32,32]{3,2,0,1:T(8,128)} copy(f32[16,1,32,32]{0,3,2,1:T(8,128)} %get-tuple-element.21) | data formatting | bytes 131072
  98.1 2.8 %copy.159 = f32[64,1,32,32]{3,2,0,1:T(8,128)} copy(f32[64,1,32,32]{0,3,2,1:T(8,128)} %get-tuple-element.19) | data formatting | bytes 524288
  100.9 3.0 %copy.158 = f32[64,1,32,32]{3,2,0,1:T(8,128)} copy(f32[64,1,32,32]{0,3,2,1:T(8,128)} %get-tuple-element.20) | data formatting | bytes 524288
  103.9 1.8 copy.157
  105.6 1.2 compare_and_fusion.7
  112.9 7.4 %fusion.2 = f32[32,16,32]{2,1,0:T(8,128)} fusion(f32[32,8,32,32]{3,2,1,0:T(8,128)} %param.18, f32[32,8,16,32]{3,2,1,0:T(8,128)} %bitcast.193, pred[32,8]{1,0:T(8,128)(4,1)} %copy.146), kind=kOutput, calls=%fused_computation.10 | convolution fusion | flops 50462720 | bytes 1638656 | tf_op jit(solution)/shard_map/tjrs,tjqs->tqr/dot_general | solution.py:140
  120.6 10.6 %all-to-all-start.1 = ((f32[64,1,512]{2,1,0:T(1,128)}), f32[64,1,512]{2,1,0:T(1,128)S(1)}, u32[]{:S(2)}, u32[]{:S(2)}) async-start(f32[64,1,512]{2,1,0:T(1,128)} %reshape.350), calls=%async_computation.1 | async-start | bytes 262144 | tf_op jit(solution)/shard_map/all_to_all | solution.py:18
  131.5 1.3 collective-permute-start.5
  132.8 1.6 gather_fusion.2
  134.4 1.6 gather_fusion.3
  136.0 1.6 gather_fusion.4
  137.6 1.6 gather_fusion.5
  139.2 1.6 gather_fusion.6
  141.3 2.3 %collective-permute-done.5 = bf16[16,32,128]{2,0,1:T(8,128)(2,1)S(1)} collective-permute-done((bf16[16,32,128]{2,0,1:T(8,128)(2,1)}, bf16[16,32,128]{2,0,1:T(8,128)(2,1)S(1)}, u32[]{:S(2)}, u32[]{:S(2)}) %collective-permute-start.5) | collective-permute-done | bytes 131104 | tf_op jit(solution)/shard_map/ppermute | solution.py:13
  144.3 1.8 gather_fusion
  158.7 1.8 fusion.10
  160.6 1.7 fusion.126
  162.3 1.9 %fusion.12 = f32[64,16,32]{2,1,0:T(8,128)S(1)} fusion(f32[64,1,32,32]{3,2,0,1:T(8,128)S(1)} %copy-done.19, f32[64,1,16,32]{3,2,1,0:T(8,128)S(1)} %reshape.351), kind=kOutput, calls=%fused_computation.28 | convolution fusion | flops 12189696 | bytes 524288 | tf_op jit(solution)/shard_map/...nrs,...nqs->...nqr/dot_general | solution.py:47
  164.3 1.7 fusion.14
  168.3 4.7 %convolution_bitcast_fusion = f32[32,16,128]{2,1,0:T(8,128)S(1)} fusion(bf16[32,8,128,128]{3,2,1,0:T(8,128)(2,1)} %all-gather.2.cloned.1.call-done, bf16[32,8,16,128]{3,2,1,0:T(8,128)(2,1)S(1)} %bitcast.195, pred[32,8]{1,0:T(8,128)(4,1)S(1)} %copy.111), kind=kOutput, calls=%fused_computation.17 | convolution fusion | flops 134742016 | bytes 9699584 | tf_op jit(solution)/shard_map/tkij,qtkj->qti/dot_general | solution.py:119
  (230 shorter events, 47.6 us)
Async XLA Ops:
  6.5 49.9 %copy-start = (f32[32,4096]{1,0:T(8,128)S(1)}, f32[32,4096]{1,0:T(8,128)}, u32[]{:S(2)}) copy-start(f32[32,4096]{1,0:T(8,128)} %param.13) | copy-start | bytes 1572868
  6.5 21.4 %copy-start.37 = (s32[32,2]{0,1:T(2,128)S(1)}, s32[32,2]{0,1:T(2,128)}, u32[]{:S(2)}) copy-start(s32[32,2]{0,1:T(2,128)} %param.15) | copy-start | bytes 772
  6.5 26.8 %copy-start.36 = (s32[32,8]{0,1:T(8,128)S(1)}, s32[32,8]{0,1:T(8,128)}, u32[]{:S(2)}) copy-start(s32[32,8]{0,1:T(8,128)} %param.17) | copy-start | bytes 3076
  6.5 26.8 %copy-start.2 = (f32[1,64,32,32]{1,3,2,0:T(8,128)S(1)}, f32[1,64,32,32]{1,3,2,0:T(8,128)}, u32[]{:S(2)}) copy-start(f32[1,64,32,32]{1,3,2,0:T(8,128)} %param.19) | copy-start | bytes 786436
  6.5 161.7 %all-gather.2.cloned.1.call-start = ((), (), s32[]{:S(2)}) async-start(), calls=%async_computation.2 | async-start | bytes 10485760 | tf_op jit(solution)/shard_map/all_gather | solution.py:114
  8.2 123.3 %collective-permute-start = (bf16[16,32,128]{2,0,1:T(8,128)(2,1)}, bf16[16,32,128]{2,0,1:T(8,128)(2,1)}, u32[]{:S(2)}, u32[]{:S(2)}) collective-permute-start(bf16[16,32,128]{2,0,1:T(8,128)(2,1)} %copy_bitcast_fusion.1), channel_id=1, source_target_pairs={{0,4},{4,8},{8,12},{12,16},{16,20},{20,24},{24,28},{28,32},{32,36}... | collective-permute-start | bytes 393224 | tf_op jit(solution)/shard_map/ppermute | solution.py:13
  10.1 124.3 %collective-permute-start.1 = (bf16[16,32,128]{2,0,1:T(8,128)(2,1)}, bf16[16,32,128]{2,0,1:T(8,128)(2,1)}, u32[]{:S(2)}, u32[]{:S(2)}) collective-permute-start(bf16[16,32,128]{2,0,1:T(8,128)(2,1)} %copy_bitcast_fusion.1), channel_id=1, source_target_pairs={{4,0},{8,4},{12,8},{16,12},{20,16},{24,20},{28,24},{32,28},{36,32}... | collective-permute-start | bytes 393224 | tf_op jit(solution)/shard_map/ppermute | solution.py:13
  13.8 122.2 %collective-permute-start.2 = (bf16[16,32,128]{2,0,1:T(8,128)(2,1)}, bf16[16,32,128]{2,0,1:T(8,128)(2,1)}, u32[]{:S(2)}, u32[]{:S(2)}) collective-permute-start(bf16[16,32,128]{2,0,1:T(8,128)(2,1)} %copy_bitcast_fusion.1), channel_id=1, source_target_pairs={{0,16},{4,20},{8,24},{12,28},{16,32},{20,36},{24,40},{28,44},{32,4... | collective-permute-start | bytes 393224 | tf_op jit(solution)/shard_map/ppermute | solution.py:13
  18.7 118.9 %collective-permute-start.3 = (bf16[16,32,128]{2,0,1:T(8,128)(2,1)}, bf16[16,32,128]{2,0,1:T(8,128)(2,1)}, u32[]{:S(2)}, u32[]{:S(2)}) collective-permute-start(bf16[16,32,128]{2,0,1:T(8,128)(2,1)} %copy_bitcast_fusion.1), channel_id=1, source_target_pairs={{16,0},{20,4},{24,8},{28,12},{32,16},{36,20},{40,24},{44,28},{48,3... | collective-permute-start | bytes 393224 | tf_op jit(solution)/shard_map/ppermute | solution.py:13
  19.9 119.2 %collective-permute-start.4 = (bf16[16,32,128]{2,0,1:T(8,128)(2,1)}, bf16[16,32,128]{2,0,1:T(8,128)(2,1)}, u32[]{:S(2)}, u32[]{:S(2)}) collective-permute-start(bf16[16,32,128]{2,0,1:T(8,128)(2,1)} %copy_bitcast_fusion.1), channel_id=1, source_target_pairs={{0,64},{4,68},{8,72},{12,76},{16,80},{20,84},{24,88},{28,92},{32,9... | collective-permute-start | bytes 393224 | tf_op jit(solution)/shard_map/ppermute | solution.py:13
  28.5 92.0 %all-to-all-start = ((s32[4,32,2]{1,2,0:T(2,128)}), s32[4,32,2]{1,2,0:T(2,128)S(1)}, u32[]{:S(2)}, u32[]{:S(2)}) async-start(s32[4,32,2]{1,2,0:T(2,128)} %stack.2), calls=%async_computation | async-start | bytes 8192 | tf_op jit(solution)/shard_map/all_to_all | solution.py:116
  34.4 4.5 %copy-start.1 = (f32[128,3,32,32]{0,3,2,1:T(8,128)S(1)}, f32[128,3,32,32]{0,3,2,1:T(8,128)}, u32[]{:S(2)}) copy-start(f32[128,3,32,32]{0,3,2,1:T(8,128)} %param.21) | copy-start | bytes 4718596
  49.7 2.8 %copy-start.35 = (s32[64,6,4]{0,2,1:T(4,128)S(1)}, s32[64,6,4]{0,2,1:T(4,128)}, u32[]{:S(2)}) copy-start(s32[64,6,4]{0,2,1:T(4,128)} %param.16) | copy-start | bytes 18436
  49.7 6.7 %copy-start.13 = (bf16[16,4096]{1,0:T(8,128)(2,1)S(1)}, bf16[16,4096]{1,0:T(8,128)(2,1)}, u32[]{:S(2)}) copy-start(bf16[16,4096]{1,0:T(8,128)(2,1)} %param.12) | copy-start | bytes 393220
  51.9 10.8 %copy-start.9 = (f32[1,8,32,32]{1,3,2,0:T(8,128)S(1)}, f32[1,8,32,32]{1,3,2,0:T(8,128)}, u32[]{:S(2)}) copy-start(f32[1,8,32,32]{1,3,2,0:T(8,128)} %slice.270) | copy-start | bytes 98308
  52.7 10.8 %copy-start.49 = (s32[4]{0:T(128)}, s32[4]{0:T(128)S(1)}, u32[]{:S(2)}) copy-start(s32[4]{0:T(128)S(1)} %get-tuple-element.12) | copy-start | bytes 52
  52.8 10.8 %copy-start.50 = (s32[4]{0:T(128)}, s32[4]{0:T(128)S(1)}, u32[]{:S(2)}) copy-start(s32[4]{0:T(128)S(1)} %get-tuple-element.13) | copy-start | bytes 52
  52.8 10.7 %copy-start.51 = (s32[4]{0:T(128)}, s32[4]{0:T(128)S(1)}, u32[]{:S(2)}) copy-start(s32[4]{0:T(128)S(1)} %get-tuple-element.14) | copy-start | bytes 52
  52.8 10.7 %copy-start.52 = (s32[4]{0:T(128)}, s32[4]{0:T(128)S(1)}, u32[]{:S(2)}) copy-start(s32[4]{0:T(128)S(1)} %get-tuple-element.15) | copy-start | bytes 52
  52.8 10.7 %copy-start.53 = (s32[4]{0:T(128)}, s32[4]{0:T(128)S(1)}, u32[]{:S(2)}) copy-start(s32[4]{0:T(128)S(1)} %get-tuple-element.16) | copy-start | bytes 52
  52.8 10.7 %copy-start.54 = (s32[4]{0:T(128)}, s32[4]{0:T(128)S(1)}, u32[]{:S(2)}) copy-start(s32[4]{0:T(128)S(1)} %get-tuple-element.17) | copy-start | bytes 52
  66.4 3.4 %copy-start.14 = (f32[1,8,32,32]{3,2,1,0:T(8,128)S(1)}, f32[1,8,32,32]{3,2,1,0:T(8,128)}, u32[]{:S(2)}) copy-start(f32[1,8,32,32]{3,2,1,0:T(8,128)} %copy.154) | copy-start | bytes 98308
  66.4 3.6 %copy-start.21 = (f32[1,4,32,32]{3,2,1,0:T(8,128)S(1)}, f32[1,4,32,32]{3,2,1,0:T(8,128)}, u32[]{:S(2)}) copy-start(f32[1,4,32,32]{3,2,1,0:T(8,128)} %copy.155) | copy-start | bytes 49156
  66.4 3.8 %copy-start.28 = (f32[1,2,32,32]{3,2,1,0:T(8,128)S(1)}, f32[1,2,32,32]{3,2,1,0:T(8,128)}, u32[]{:S(2)}) copy-start(f32[1,2,32,32]{3,2,1,0:T(8,128)} %copy.156) | copy-start | bytes 24580
  69.4 6.5 %copy-start.12 = (f32[32,1,32,32]{0,3,2,1:T(8,128)S(1)}, f32[32,1,32,32]{0,3,2,1:T(8,128)}, u32[]{:S(2)}) copy-start(f32[32,1,32,32]{0,3,2,1:T(8,128)} %get-tuple-element.30) | copy-start | bytes 393220
  77.1 11.2 %copy-start.8 = (f32[8,32,32]{0,2,1:T(8,128)S(1)}, f32[8,32,32]{0,2,1:T(8,128)}, u32[]{:S(2)}) copy-start(f32[8,32,32]{0,2,1:T(8,128)} %slice.319) | copy-start | bytes 98308
  89.1 6.0 %copy-start.11 = (f32[16,1,32,32]{0,3,2,1:T(8,128)S(1)}, f32[16,1,32,32]{0,3,2,1:T(8,128)}, u32[]{:S(2)}) copy-start(f32[16,1,32,32]{0,3,2,1:T(8,128)} %get-tuple-element.23) | copy-start | bytes 196612
  96.0 7.8 %copy-start.10 = (f32[64,1,32,32]{0,3,2,1:T(8,128)S(1)}, f32[64,1,32,32]{0,3,2,1:T(8,128)}, u32[]{:S(2)}) copy-start(f32[64,1,32,32]{0,3,2,1:T(8,128)} %get-tuple-element.18) | copy-start | bytes 786436
  112.8 28.0 %copy-start.48 = (pred[4]{0:T(512)(128)(4,1)S(1)}, pred[4]{0:T(512)(128)(4,1)}, u32[]{:S(2)}) copy-start(pred[4]{0:T(512)(128)(4,1)} %compare_and_fusion.7) | copy-start | bytes 16
  112.8 28.0 %copy-start.47 = (pred[4]{0:T(512)(128)(4,1)S(1)}, pred[4]{0:T(512)(128)(4,1)}, u32[]{:S(2)}) copy-start(pred[4]{0:T(512)(128)(4,1)} %compare_and_fusion.6) | copy-start | bytes 16
  112.9 28.1 %copy-start.46 = (pred[4]{0:T(512)(128)(4,1)S(1)}, pred[4]{0:T(512)(128)(4,1)}, u32[]{:S(2)}) copy-start(pred[4]{0:T(512)(128)(4,1)} %compare_and_fusion.5) | copy-start | bytes 16
  112.9 28.2 %copy-start.45 = (pred[4]{0:T(512)(128)(4,1)S(1)}, pred[4]{0:T(512)(128)(4,1)}, u32[]{:S(2)}) copy-start(pred[4]{0:T(512)(128)(4,1)} %compare_and_fusion.4) | copy-start | bytes 16
  112.9 28.3 %copy-start.44 = (pred[4]{0:T(512)(128)(4,1)S(1)}, pred[4]{0:T(512)(128)(4,1)}, u32[]{:S(2)}) copy-start(pred[4]{0:T(512)(128)(4,1)} %compare_and_fusion.3) | copy-start | bytes 16
  112.9 31.3 %copy-start.43 = (pred[4]{0:T(512)(128)(4,1)S(1)}, pred[4]{0:T(512)(128)(4,1)}, u32[]{:S(2)}) copy-start(pred[4]{0:T(512)(128)(4,1)} %compare_and_fusion.2) | copy-start | bytes 16
  120.6 25.6 %all-to-all-start.1 = ((f32[64,1,512]{2,1,0:T(1,128)}), f32[64,1,512]{2,1,0:T(1,128)S(1)}, u32[]{:S(2)}, u32[]{:S(2)}) async-start(f32[64,1,512]{2,1,0:T(1,128)} %reshape.350), calls=%async_computation.1 | async-start | bytes 262144 | tf_op jit(solution)/shard_map/all_to_all | solution.py:18
  131.5 12.0 %collective-permute-start.5 = (bf16[16,32,128]{2,0,1:T(8,128)(2,1)}, bf16[16,32,128]{2,0,1:T(8,128)(2,1)S(1)}, u32[]{:S(2)}, u32[]{:S(2)}) collective-permute-start(bf16[16,32,128]{2,0,1:T(8,128)(2,1)} %copy_bitcast_fusion.1), channel_id=1, source_target_pairs={{64,0},{68,4},{72,8},{76,12},{80,16},{84,20},{88,24},{92,28},{96,3... | collective-permute-start | bytes 393224 | tf_op jit(solution)/shard_map/ppermute | solution.py:13
  147.8 2.2 %copy-start.16 = (f32[8,32,32]{2,1,0:T(8,128)S(1)}, f32[8,32,32]{2,1,0:T(8,128)}, u32[]{:S(2)}) copy-start(f32[8,32,32]{2,1,0:T(8,128)} %copy.172) | copy-start | bytes 98308
  148.9 2.5 %copy-start.25 = (f32[8,1,32,32]{3,2,0,1:T(8,128)S(1)}, f32[8,1,32,32]{3,2,0,1:T(8,128)}, u32[]{:S(2)}) copy-start(f32[8,1,32,32]{3,2,0,1:T(8,128)} %copy.169) | copy-start | bytes 98308
  148.9 2.8 %copy-start.23 = (f32[8,1,32,32]{3,2,0,1:T(8,128)S(1)}, f32[8,1,32,32]{3,2,0,1:T(8,128)}, u32[]{:S(2)}) copy-start(f32[8,1,32,32]{3,2,0,1:T(8,128)} %copy.170) | copy-start | bytes 98308
  149.0 3.4 %copy-start.18 = (f32[16,1,32,32]{3,2,0,1:T(8,128)S(1)}, f32[16,1,32,32]{3,2,0,1:T(8,128)}, u32[]{:S(2)}) copy-start(f32[16,1,32,32]{3,2,0,1:T(8,128)} %copy.167) | copy-start | bytes 196612
  149.0 3.4 %copy-start.40 = (pred[16]{0:T(512)(128)(4,1)S(1)}, pred[16]{0:T(512)(128)(4,1)}, u32[]{:S(2)}) copy-start(pred[16]{0:T(512)(128)(4,1)} %fusion.103) | copy-start | bytes 52
  149.6 3.9 %copy-start.30 = (f32[16,1,32,32]{3,2,0,1:T(8,128)S(1)}, f32[16,1,32,32]{3,2,0,1:T(8,128)}, u32[]{:S(2)}) copy-start(f32[16,1,32,32]{3,2,0,1:T(8,128)} %copy.165) | copy-start | bytes 196612
  150.2 3.8 %copy-start.31 = (f32[16,1,32,32]{3,2,0,1:T(8,128)S(1)}, f32[16,1,32,32]{3,2,0,1:T(8,128)}, u32[]{:S(2)}) copy-start(f32[16,1,32,32]{3,2,0,1:T(8,128)} %copy.166) | copy-start | bytes 196612
  151.7 2.9 %copy-start.26 = (f32[32,1,32,32]{3,2,0,1:T(8,128)S(1)}, f32[32,1,32,32]{3,2,0,1:T(8,128)}, u32[]{:S(2)}) copy-start(f32[32,1,32,32]{3,2,0,1:T(8,128)} %copy.161) | copy-start | bytes 393220
  158.7 3.6 %copy-start.19 = (f32[64,1,32,32]{3,2,0,1:T(8,128)S(1)}, f32[64,1,32,32]{3,2,0,1:T(8,128)}, u32[]{:S(2)}) copy-start(f32[64,1,32,32]{3,2,0,1:T(8,128)} %copy.158) | copy-start | bytes 786436
  164.2 2.2 %copy-start.15 = (f32[1,8,32,32]{3,2,1,0:T(8,128)S(1)}, f32[1,8,32,32]{3,2,1,0:T(8,128)}, u32[]{:S(2)}) copy-start(f32[1,8,32,32]{3,2,1,0:T(8,128)} %copy.154) | copy-start | bytes 98308
  164.3 3.1 %copy-start.17 = (f32[32,16,32]{2,1,0:T(8,128)S(1)}, f32[32,16,32]{2,1,0:T(8,128)}, u32[]{:S(2)}) copy-start(f32[32,16,32]{2,1,0:T(8,128)} %fusion.2) | copy-start | bytes 196612
  166.0 2.3 %copy-start.5 = (bf16[256,16,128]{2,1,0:T(8,128)(2,1)S(1)}, bf16[256,16,128]{2,1,0:T(8,128)(2,1)}, u32[]{:S(2)}) copy-start(bf16[256,16,128]{2,1,0:T(8,128)(2,1)} %gather_fusion) | copy-start | bytes 3145732
  (16 other events, 26.8 us)
Sparse Core Ops, SparseCore 0:
  28.0 86.9 all-gather.1
